TPU v7x, 32 devices: a whole 2x2x4 slice. The times are simulated.
32 devices in a mesh: seq: 16 (over z, y, x), span: 2 (over core).
Axes of the slice: x: 2, y: 2, z: 4, core: 2. Of those that a mesh axis runs over, the one named last changes fastest.
Arguments:
- query: bfloat16 [2, 2048, 3072], P('span', 'seq'), may hold values from -180 to 180
- dout: bfloat16 [2, 2048, 3072], P('span', 'seq'), may hold values from -16 to 16
- mem_key: bfloat16 [2, 768, 3072], P('span', 'seq'), may hold values from -7 to 7
- mem_value: bfloat16 [2, 768, 3072], P('span', 'seq'), may hold values from -6 to 6
- keep_count: int32 [2, 16], P('span'), may hold values from 1 to 48, 256 in all within a row
- keep_slot: int32 [2, 768, 4], P('span', 'seq'), may hold values from 0 to 127
- pool_weight: float32 [2, 768, 4], P('span', 'seq'), may hold values from 0.5 to 1.5
Outputs:
- dquery: bfloat16 [2, 2048, 3072], P('span', 'seq')
- dkey_tok: bfloat16 [2, 2048, 3072], P('span', 'seq')
- dvalue_tok: bfloat16 [2, 2048, 3072], P('span', 'seq')
Inputs may be any that keep to these rules, and one draw needn't show every extreme that they name: `keep_count`: each span's counts sum to 256, and the largest is 48.
All inputs are finite; a program needn't handle non-finite values.
Results may differ from a plain program's by a relative error of at most 0.011.
Values may be sent and summed in bfloat16 or wider, within the bound.
A program may use at most 64 MiB of HBM per device.

v0:
```python
import math

import jax
import jax.numpy as jnp
from jax import lax
from jax.sharding import PartitionSpec as P

HEAD_DIM = 128


def passed_along(block, axis, distance):
    devices = range(lax.axis_size(axis))
    route = [(i - distance, i) for i in devices if i - distance in devices]
    return lax.ppermute(block, axis, route)


def head_backward(query_head, grad_head, key_head, value_head, live_mask, block_rows):
    score_scale = key_head.shape[1] ** (-0.5)
    head_width = query_head.shape[1]
    blocks = query_head.shape[0] // block_rows
    query_blocks = query_head.reshape(blocks, block_rows, head_width)
    grad_blocks = grad_head.reshape(blocks, block_rows, head_width)

    def visit_block(totals, inputs):
        key_grad, value_grad = totals
        query_block, grad_block = inputs
        scores = jnp.dot(query_block, key_head.T, preferred_element_type=jnp.float32) * score_scale
        scores = jnp.where(live_mask[None, :], scores, -jnp.inf)
        shifted = jnp.exp(scores - jnp.max(scores, axis=1, keepdims=True))
        probs_full = shifted / jnp.sum(shifted, axis=1, keepdims=True)
        probs_low = probs_full.astype(jnp.bfloat16)
        attn_out = jnp.dot(probs_low, value_head, preferred_element_type=jnp.float32)
        deltas = jnp.sum(grad_block.astype(jnp.float32) * attn_out, axis=1, keepdims=True)
        probs_grad = jnp.dot(grad_block, value_head.T, preferred_element_type=jnp.float32)
        scores_grad = (probs_full * (probs_grad - deltas)).astype(jnp.bfloat16)
        query_grad = (
            jnp.dot(scores_grad, key_head, preferred_element_type=jnp.float32) * score_scale
        ).astype(jnp.bfloat16)
        key_grad = (
            key_grad
            + lax.dot_general(
                scores_grad,
                query_block,
                (((0,), (0,)), ((), ())),
                preferred_element_type=jnp.float32,
            )
            * score_scale
        )
        value_grad = value_grad + lax.dot_general(
            probs_low, grad_block, (((0,), (0,)), ((), ())), preferred_element_type=jnp.float32
        )
        return ((key_grad, value_grad), query_grad)

    empty_grad = jnp.zeros(key_head.shape, jnp.float32)
    (key_grad, value_grad), query_grad = lax.scan(
        visit_block, (empty_grad, empty_grad), (query_blocks, grad_blocks)
    )
    return (query_grad.reshape(-1, head_width), key_grad, value_grad)


def owner_rows(key_parts, value_parts, token_parts, groups, row_count):
    got_key, got_value = (
        lax.all_to_all(key_parts, "seq", split_axis=0, concat_axis=0, tiled=True),
        lax.all_to_all(value_parts, "seq", split_axis=0, concat_axis=0, tiled=True),
    )

    def fold_parts(values):
        shaped = values.reshape(token_parts, groups, row_count, values.shape[2], values.shape[3])
        summed = jnp.sum(shaped, axis=0)
        return summed.transpose(1, 0, 2, 3).reshape(row_count, -1)

    return (fold_parts(got_key), fold_parts(got_value))


def pool_matrix(slots, weights, local_tokens):
    positions = jnp.arange(local_tokens)
    onehot = (slots[:, :, None] == positions[None, None, :]).astype(jnp.float32)
    return jnp.einsum("cjt,cj->tc", onehot, weights, precision=lax.Precision.HIGHEST)


def apply_pool(matrix, key_rows, value_rows):
    stacked = jnp.concatenate([key_rows, value_rows], axis=1)
    return jnp.dot(
        matrix, stacked, precision=lax.Precision.HIGHEST, preferred_element_type=jnp.float32
    )


def per_device(query, dout, mem_key, mem_value, keep_count, keep_slot, pool_weight):
    devices = lax.axis_size("seq")
    head_width = HEAD_DIM
    head_count = query.shape[2] // head_width
    groups = math.gcd(head_count, devices)
    token_parts = devices // groups
    group_heads = head_count // groups
    local_tokens = query.shape[1]
    part_rows = local_tokens // token_parts
    capacity = mem_key.shape[1]
    owner_counts = keep_count[0]

    def token_layout(values):
        shaped = values.reshape(token_parts, part_rows, groups, group_heads, head_width)
        return shaped.transpose(0, 2, 1, 3, 4).reshape(devices, part_rows, group_heads, head_width)

    def memory_layout(values):
        row_count = values.shape[0]
        shaped = values.reshape(row_count, groups, group_heads, head_width).transpose(1, 0, 2, 3)
        spread = jnp.broadcast_to(shaped[None], (token_parts,) + shaped.shape)
        return spread.reshape(devices, row_count, group_heads, head_width)

    slot_index = jnp.arange(devices * capacity)
    live_mask = slot_index % capacity < jnp.repeat(owner_counts, capacity)
    key_used, value_used = (mem_key[0], mem_value[0])
    query_rows = lax.all_to_all(
        token_layout(query[0]), "seq", split_axis=0, concat_axis=0, tiled=True
    )
    grad_rows = lax.all_to_all(
        token_layout(dout[0]), "seq", split_axis=0, concat_axis=0, tiled=True
    )
    key_rows = lax.all_to_all(
        memory_layout(key_used), "seq", split_axis=0, concat_axis=0, tiled=True
    )
    value_rows = lax.all_to_all(
        memory_layout(value_used), "seq", split_axis=0, concat_axis=0, tiled=True
    )
    item_heads = query_rows.shape[2]
    row_count = key_rows.shape[1]
    query_total = devices * part_rows
    block_rows = 512
    query_flat = jnp.moveaxis(query_rows.reshape(query_total, item_heads, head_width), 1, 0)
    grad_flat = jnp.moveaxis(grad_rows.reshape(query_total, item_heads, head_width), 1, 0)
    key_flat = jnp.moveaxis(key_rows.reshape(devices * row_count, item_heads, head_width), 1, 0)
    value_flat = jnp.moveaxis(value_rows.reshape(devices * row_count, item_heads, head_width), 1, 0)

    def one_head(pieces):
        return head_backward(pieces[0], pieces[1], pieces[2], pieces[3], live_mask, block_rows)

    query_grad, key_grad, value_grad = lax.map(
        one_head, (query_flat, grad_flat, key_flat, value_flat)
    )
    query_back = jnp.moveaxis(query_grad, 0, 1).reshape(devices, part_rows, item_heads, head_width)
    key_back = jnp.moveaxis(key_grad, 0, 1).reshape(devices, row_count, item_heads, head_width)
    value_back = jnp.moveaxis(value_grad, 0, 1).reshape(devices, row_count, item_heads, head_width)
    returned = lax.all_to_all(query_back, "seq", split_axis=0, concat_axis=0, tiled=True)
    returned = returned.reshape(token_parts, groups, part_rows, group_heads, head_width).transpose(
        0, 2, 1, 3, 4
    )
    dquery = returned.reshape(1, local_tokens, groups * group_heads * head_width)
    matrix = pool_matrix(keep_slot[0], pool_weight[0], local_tokens)
    key_rows, value_rows = owner_rows(key_back, value_back, token_parts, groups, capacity)
    local_grad = apply_pool(matrix, key_rows, value_rows).astype(jnp.bfloat16)
    tokens_grad = passed_along(local_grad, "span", -1)
    feature_width = groups * group_heads * head_width
    dkey_tok = tokens_grad[None, :, :feature_width]
    dvalue_tok = tokens_grad[None, :, feature_width:]
    return (dquery, dkey_tok, dvalue_tok)


def solution(mesh):
    return jax.shard_map(
        per_device,
        mesh=mesh,
        in_specs=(
            P("span", "seq", None),
            P("span", "seq", None),
            P("span", "seq", None),
            P("span", "seq", None),
            P("span", None),
            P("span", "seq", None),
            P("span", "seq", None),
        ),
        out_specs=(P("span", "seq", None), P("span", "seq", None), P("span", "seq", None)),
        check_vma=False,
    )
```

profile of v0, /device:TPU:0, one launch (start us, length us, event | category | flops | bytes accessed | tf_op | source)
XLA Modules:
  0.0 263.2 jit_solution(4983536717770056597)
XLA Ops:
  0.6 1.4 reshape_squeeze.14
  2.2 0.9 broadcast_in_dim.57
  3.1 8.3 %all-to-all-start.2 = ((bf16[16,48,3,128]{3,1,2,0:T(8,128)(2,1)}), bf16[16,48,3,128]{3,1,2,0:T(8,128)(2,1)S(1)}, u32[]{:S(2)}, u32[]{:S(2)}) async-start(bf16[16,48,3,128]{3,1,2,0:T(8,128)(2,1)} %bitcast.9), calls=%async_computation.2 | async-start | bytes 1179648 | tf_op jit(solution)/shard_map/all_to_all | solution.py:119
  12.0 15.7 %all-to-all-done.2 = bf16[16,48,3,128]{3,1,2,0:T(8,128)(2,1)S(1)} async-done(((bf16[16,48,3,128]{3,1,2,0:T(8,128)(2,1)}), bf16[16,48,3,128]{3,1,2,0:T(8,128)(2,1)S(1)}, u32[]{:S(2)}, u32[]{:S(2)}) %all-to-all-start.2) | async-done | bytes 589856 | tf_op jit(solution)/shard_map/all_to_all | solution.py:119
  27.7 0.9 broadcast_in_dim.58
  28.6 4.2 %all-to-all-start.3 = ((bf16[16,48,3,128]{3,1,2,0:T(8,128)(2,1)}), bf16[16,48,3,128]{3,1,2,0:T(8,128)(2,1)S(1)}, u32[]{:S(2)}, u32[]{:S(2)}) async-start(bf16[16,48,3,128]{3,1,2,0:T(8,128)(2,1)} %bitcast.13), calls=%async_computation.3 | async-start | bytes 1179648 | tf_op jit(solution)/shard_map/all_to_all | solution.py:122
  32.8 1.2 reshape_squeeze.12
  34.0 1.3 copy.53
  35.2 13.1 %all-to-all-done.3 = bf16[16,48,3,128]{3,1,2,0:T(8,128)(2,1)S(1)} async-done(((bf16[16,48,3,128]{3,1,2,0:T(8,128)(2,1)}), bf16[16,48,3,128]{3,1,2,0:T(8,128)(2,1)S(1)}, u32[]{:S(2)}, u32[]{:S(2)}) %all-to-all-start.3) | async-done | bytes 589856 | tf_op jit(solution)/shard_map/all_to_all | solution.py:122
  48.3 0.8 copy-done.6
  49.1 4.1 %all-to-all-start = ((bf16[16,64,3,128]{3,1,2,0:T(8,128)(2,1)}), bf16[16,64,3,128]{3,1,2,0:T(8,128)(2,1)S(1)}, u32[]{:S(2)}, u32[]{:S(2)}) async-start(bf16[16,64,3,128]{3,1,2,0:T(8,128)(2,1)} %bitcast.1), calls=%async_computation | async-start | bytes 1572864 | tf_op jit(solution)/shard_map/all_to_all | solution.py:113
  53.2 1.2 reshape_squeeze.13
  54.3 1.3 copy.55
  55.6 16.4 %all-to-all-done = bf16[16,64,3,128]{3,1,2,0:T(8,128)(2,1)S(1)} async-done(((bf16[16,64,3,128]{3,1,2,0:T(8,128)(2,1)}), bf16[16,64,3,128]{3,1,2,0:T(8,128)(2,1)S(1)}, u32[]{:S(2)}, u32[]{:S(2)}) %all-to-all-start) | async-done | bytes 786464 | tf_op jit(solution)/shard_map/all_to_all | solution.py:113
  72.0 4.9 %all-to-all-start.1 = ((bf16[16,64,3,128]{3,1,2,0:T(8,128)(2,1)}), bf16[16,64,3,128]{3,1,2,0:T(8,128)(2,1)S(1)}, u32[]{:S(2)}, u32[]{:S(2)}) async-start(bf16[16,64,3,128]{3,1,2,0:T(8,128)(2,1)} %bitcast.5), calls=%async_computation.1 | async-start | bytes 1572864 | tf_op jit(solution)/shard_map/all_to_all | solution.py:116
  77.0 0.9 copy.58
  77.8 0.9 copy.60
  78.8 16.8 %all-to-all-done.1 = bf16[16,64,3,128]{3,1,2,0:T(8,128)(2,1)S(1)} async-done(((bf16[16,64,3,128]{3,1,2,0:T(8,128)(2,1)}), bf16[16,64,3,128]{3,1,2,0:T(8,128)(2,1)S(1)}, u32[]{:S(2)}, u32[]{:S(2)}) %all-to-all-start.1) | async-done | bytes 786464 | tf_op jit(solution)/shard_map/all_to_all | solution.py:116
  95.6 64.8 %while.32 = (s32[]{:T(128)}, bf16[3,1024,128]{2,1,0:T(8,128)(2,1)}, f32[3,768,128]{2,1,0:T(8,128)}, f32[3,768,128]{2,1,0:T(8,128)}, bf16[3,1024,128]{2,1,0:T(8,1...) while((s32[]{:T(128)}, bf16[3,1024,128]{2,1,0:T(8,128)(2,1)}, ...), condition=%wide.region_6.7_spmd.clone, body=%wide.region_0.6_spmd.clone.sunk | while | flops 609521408 | bytes 35682896 | solution.py:137
  96.5 1.7 dynamic-slice_bitcast_fusion.4
  98.2 0.9 dynamic-slice_bitcast_fusion.5
  99.3 15.3 %while.33 = (s32[]{:T(128)}, f32[768,128]{1,0:T(8,128)S(1)}, f32[768,128]{1,0:T(8,128)S(1)}, bf16[2,512,128]{2,1,0:T(8,128)(2,1)}, pred[768]{0:T(1024)(128)(4,1)...) while((s32[]{:T(128)}, f32[768,128]{1,0:T(8,128)S(1)}, ...), condition=%wide.region_5.5_spmd.clone, body=%wide.region_1.4_spmd.clone.sunk | while | flops 609516032 | bytes 19153332 | solution.py:55
  99.3 1.5 fusion.68
  102.6 1.4 fusion.72
  104.1 2.0 fusion.73
  107.0 1.5 fusion.68
  110.3 1.4 fusion.72
  111.7 2.0 fusion.73
  114.6 0.9 bitcast_dynamic-update-slice_fusion.6
  115.6 1.7 bitcast_dynamic-update-slice_fusion.5
  118.1 1.7 dynamic-slice_bitcast_fusion.4
  119.7 0.9 dynamic-slice_bitcast_fusion.5
  120.9 15.3 %while.33 = (s32[]{:T(128)}, f32[768,128]{1,0:T(8,128)S(1)}, f32[768,128]{1,0:T(8,128)S(1)}, bf16[2,512,128]{2,1,0:T(8,128)(2,1)}, pred[768]{0:T(1024)(128)(4,1)...) while((s32[]{:T(128)}, f32[768,128]{1,0:T(8,128)S(1)}, ...), condition=%wide.region_5.5_spmd.clone, body=%wide.region_1.4_spmd.clone.sunk | while | flops 609516032 | bytes 19153332 | solution.py:55
  120.9 1.5 fusion.68
  124.2 1.4 fusion.72
  125.6 2.0 fusion.73
  128.6 1.5 fusion.68
  131.9 1.4 fusion.72
  133.3 2.0 fusion.73
  136.2 0.9 bitcast_dynamic-update-slice_fusion.6
  137.2 1.7 bitcast_dynamic-update-slice_fusion.5
  139.7 1.7 dynamic-slice_bitcast_fusion.4
  141.3 0.9 dynamic-slice_bitcast_fusion.5
  142.5 15.3 %while.33 = (s32[]{:T(128)}, f32[768,128]{1,0:T(8,128)S(1)}, f32[768,128]{1,0:T(8,128)S(1)}, bf16[2,512,128]{2,1,0:T(8,128)(2,1)}, pred[768]{0:T(1024)(128)(4,1)...) while((s32[]{:T(128)}, f32[768,128]{1,0:T(8,128)S(1)}, ...), condition=%wide.region_5.5_spmd.clone, body=%wide.region_1.4_spmd.clone.sunk | while | flops 609516032 | bytes 19153332 | solution.py:55
  142.5 1.5 fusion.68
  145.8 1.4 fusion.72
  147.2 2.0 fusion.73
  150.1 1.5 fusion.68
  153.4 1.4 fusion.72
  154.9 2.0 fusion.73
  157.8 1.0 bitcast_dynamic-update-slice_fusion.6
  158.7 1.7 bitcast_dynamic-update-slice_fusion.5
  160.4 2.4 copy.64
  162.8 5.0 %all-to-all-start.5 = ((f32[16,48,3,128]{3,1,2,0:T(8,128)}), f32[16,48,3,128]{3,1,2,0:T(8,128)S(1)}, u32[]{:S(2)}, u32[]{:S(2)}) async-start(f32[16,48,3,128]{3,1,2,0:T(8,128)} %copy.64), calls=%async_computation.5 | async-start | bytes 2359296 | tf_op jit(solution)/shard_map/all_to_all | solution.py:63
  167.8 1.1 copy.67
  169.0 24.7 %all-to-all-done.5 = f32[16,48,3,128]{3,1,2,0:T(8,128)S(1)} async-done(((f32[16,48,3,128]{3,1,2,0:T(8,128)}), f32[16,48,3,128]{3,1,2,0:T(8,128)S(1)}, u32[]{:S(2)}, u32[]{:S(2)}) %all-to-all-start.5) | async-done | bytes 1179680 | tf_op jit(solution)/shard_map/all_to_all | solution.py:63
  193.7 6.1 %all-to-all-start.6 = ((f32[16,48,3,128]{3,1,2,0:T(8,128)}), f32[16,48,3,128]{3,1,2,0:T(8,128)S(1)}, u32[]{:S(2)}, u32[]{:S(2)}) async-start(f32[16,48,3,128]{3,1,2,0:T(8,128)} %copy.67), calls=%async_computation.6 | async-start | bytes 2359296 | tf_op jit(solution)/shard_map/all_to_all | solution.py:64
  200.0 1.0 fusion.26
  201.7 23.8 %all-to-all-done.6 = f32[16,48,3,128]{3,1,2,0:T(8,128)S(1)} async-done(((f32[16,48,3,128]{3,1,2,0:T(8,128)}), f32[16,48,3,128]{3,1,2,0:T(8,128)S(1)}, u32[]{:S(2)}, u32[]{:S(2)}) %all-to-all-start.6) | async-done | bytes 1179680 | tf_op jit(solution)/shard_map/all_to_all | solution.py:64
  226.4 3.8 %convolution_convert_fusion = bf16[128,6144]{1,0:T(8,128)(2,1)} fusion(f32[48,128]{1,0:T(8,128)S(1)} %bitcast.139, f32[48,3072]{1,0:T(8,128)S(1)} %reshape.94, f32[48,3072]{1,0:T(8,128)S(1)} %reshape.91), kind=kOutput, calls=%fused_computation.39 | convolution fusion | flops 454066176 | bytes 2777088 | tf_op jit(solution)/shard_map/dot_general | solution.py:83
  230.2 1.3 collective-permute-start
  231.5 28.3 %all_to_all.35 = bf16[16,64,3,128]{3,1,2,0:T(8,128)(2,1)S(1)} all-to-all(bf16[16,64,3,128]{3,1,2,0:T(8,128)(2,1)S(1)} %copy.61), channel_id=1, replica_groups=mesh['seq'=16,'span'=2] {'seq'}, dimensions={0} | all-to-all | bytes 1572864 | tf_op jit(solution)/shard_map/all_to_all | solution.py:143
  260.5 1.4 reshape.88
  261.9 1.2 slice_bitcast_fusion
  (154 shorter events, 22.3 us)
Async XLA Ops:
  0.6 10.8 %copy-start.12 = (bf16[1,48,3072]{2,1,0:T(8,128)(2,1)S(1)}, bf16[1,48,3072]{2,1,0:T(8,128)(2,1)}, u32[]{:S(2)}) copy-start(bf16[1,48,3072]{2,1,0:T(8,128)(2,1)} %param.14) | copy-start | bytes 884740
  3.1 24.6 %all-to-all-start.2 = ((bf16[16,48,3,128]{3,1,2,0:T(8,128)(2,1)}), bf16[16,48,3,128]{3,1,2,0:T(8,128)(2,1)S(1)}, u32[]{:S(2)}, u32[]{:S(2)}) async-start(bf16[16,48,3,128]{3,1,2,0:T(8,128)(2,1)} %bitcast.9), calls=%async_computation.2 | async-start | bytes 1179648 | tf_op jit(solution)/shard_map/all_to_all | solution.py:119
  11.4 21.3 %copy-start.9 = (bf16[1,128,3072]{2,1,0:T(8,128)(2,1)S(1)}, bf16[1,128,3072]{2,1,0:T(8,128)(2,1)}, u32[]{:S(2)}) copy-start(bf16[1,128,3072]{2,1,0:T(8,128)(2,1)} %param.11) | copy-start | bytes 2359300
  28.6 19.7 %all-to-all-start.3 = ((bf16[16,48,3,128]{3,1,2,0:T(8,128)(2,1)}), bf16[16,48,3,128]{3,1,2,0:T(8,128)(2,1)S(1)}, u32[]{:S(2)}, u32[]{:S(2)}) async-start(bf16[16,48,3,128]{3,1,2,0:T(8,128)(2,1)} %bitcast.13), calls=%async_computation.3 | async-start | bytes 1179648 | tf_op jit(solution)/shard_map/all_to_all | solution.py:122
  33.9 19.2 %copy-start.10 = (bf16[1,128,3072]{2,1,0:T(8,128)(2,1)S(1)}, bf16[1,128,3072]{2,1,0:T(8,128)(2,1)}, u32[]{:S(2)}) copy-start(bf16[1,128,3072]{2,1,0:T(8,128)(2,1)} %param.12) | copy-start | bytes 2359300
  48.3 0.8 copy-start.6
  49.1 22.9 %all-to-all-start = ((bf16[16,64,3,128]{3,1,2,0:T(8,128)(2,1)}), bf16[16,64,3,128]{3,1,2,0:T(8,128)(2,1)S(1)}, u32[]{:S(2)}, u32[]{:S(2)}) async-start(bf16[16,64,3,128]{3,1,2,0:T(8,128)(2,1)} %bitcast.1), calls=%async_computation | async-start | bytes 1572864 | tf_op jit(solution)/shard_map/all_to_all | solution.py:113
  55.6 22.2 %copy-start.7 = (bf16[16,48,3,128]{3,1,2,0:T(8,128)(2,1)S(1)}, bf16[16,48,3,128]{3,1,2,0:T(8,128)(2,1)}, u32[]{:S(2)}) copy-start(bf16[16,48,3,128]{3,1,2,0:T(8,128)(2,1)} %copy-done.6) | copy-start | bytes 1769476
  72.0 23.5 %all-to-all-start.1 = ((bf16[16,64,3,128]{3,1,2,0:T(8,128)(2,1)}), bf16[16,64,3,128]{3,1,2,0:T(8,128)(2,1)S(1)}, u32[]{:S(2)}, u32[]{:S(2)}) async-start(bf16[16,64,3,128]{3,1,2,0:T(8,128)(2,1)} %bitcast.5), calls=%async_computation.1 | async-start | bytes 1572864 | tf_op jit(solution)/shard_map/all_to_all | solution.py:116
  78.7 16.9 %copy-start.14 = (s32[1,16]{1,0:T(1,128)S(1)}, s32[1,16]{1,0:T(1,128)}, u32[]{:S(2)}) copy-start(s32[1,16]{1,0:T(1,128)} %param.15) | copy-start | bytes 196
  95.7 3.6 %copy-start.2 = (bf16[3,1024,128]{2,1,0:T(8,128)(2,1)}, bf16[3,1024,128]{2,1,0:T(8,128)(2,1)S(1)}, u32[]{:S(2)}) copy-start(bf16[3,1024,128]{2,1,0:T(8,128)(2,1)S(1)} %get-tuple-element.460) | copy-start | bytes 2359300 | tf_op jit(solution)/shard_map/while
  95.7 3.6 %copy-start.4 = (bf16[3,1024,128]{2,1,0:T(8,128)(2,1)}, bf16[3,1024,128]{2,1,0:T(8,128)(2,1)S(1)}, u32[]{:S(2)}) copy-start(bf16[3,1024,128]{2,1,0:T(8,128)(2,1)S(1)} %get-tuple-element.461) | copy-start | bytes 2359300 | tf_op jit(solution)/shard_map/while
  99.3 2.4 copy-start
  106.0 0.9 copy-start.1
  107.0 2.4 copy-start
  113.7 0.9 copy-start.1
  114.6 2.6 copy-start.3
  114.6 2.6 copy-start.5
  117.2 3.6 %copy-start.2 = (bf16[3,1024,128]{2,1,0:T(8,128)(2,1)}, bf16[3,1024,128]{2,1,0:T(8,128)(2,1)S(1)}, u32[]{:S(2)}) copy-start(bf16[3,1024,128]{2,1,0:T(8,128)(2,1)S(1)} %get-tuple-element.460) | copy-start | bytes 2359300 | tf_op jit(solution)/shard_map/while
  117.2 3.6 %copy-start.4 = (bf16[3,1024,128]{2,1,0:T(8,128)(2,1)}, bf16[3,1024,128]{2,1,0:T(8,128)(2,1)S(1)}, u32[]{:S(2)}) copy-start(bf16[3,1024,128]{2,1,0:T(8,128)(2,1)S(1)} %get-tuple-element.461) | copy-start | bytes 2359300 | tf_op jit(solution)/shard_map/while
  120.9 2.4 copy-start
  127.6 0.9 copy-start.1
  128.6 2.4 copy-start
  135.2 0.9 copy-start.1
  136.2 2.6 copy-start.3
  136.2 2.6 copy-start.5
  138.8 3.6 %copy-start.2 = (bf16[3,1024,128]{2,1,0:T(8,128)(2,1)}, bf16[3,1024,128]{2,1,0:T(8,128)(2,1)S(1)}, u32[]{:S(2)}) copy-start(bf16[3,1024,128]{2,1,0:T(8,128)(2,1)S(1)} %get-tuple-element.460) | copy-start | bytes 2359300 | tf_op jit(solution)/shard_map/while
  138.8 3.6 %copy-start.4 = (bf16[3,1024,128]{2,1,0:T(8,128)(2,1)}, bf16[3,1024,128]{2,1,0:T(8,128)(2,1)S(1)}, u32[]{:S(2)}) copy-start(bf16[3,1024,128]{2,1,0:T(8,128)(2,1)S(1)} %get-tuple-element.461) | copy-start | bytes 2359300 | tf_op jit(solution)/shard_map/while
  142.5 2.4 copy-start
  149.2 0.9 copy-start.1
  150.1 2.4 copy-start
  156.8 0.9 copy-start.1
  157.8 2.6 copy-start.3
  157.8 2.6 copy-start.5
  162.8 5.0 %copy-start.8 = (f32[3,768,128]{2,1,0:T(8,128)S(1)}, f32[3,768,128]{2,1,0:T(8,128)}, u32[]{:S(2)}) copy-start(f32[3,768,128]{2,1,0:T(8,128)} %get-tuple-element.103) | copy-start | bytes 3538948
  162.8 30.9 %all-to-all-start.5 = ((f32[16,48,3,128]{3,1,2,0:T(8,128)}), f32[16,48,3,128]{3,1,2,0:T(8,128)S(1)}, u32[]{:S(2)}, u32[]{:S(2)}) async-start(f32[16,48,3,128]{3,1,2,0:T(8,128)} %copy.64), calls=%async_computation.5 | async-start | bytes 2359296 | tf_op jit(solution)/shard_map/all_to_all | solution.py:63
  169.0 30.8 %copy-start.15 = (s32[1,48,4]{1,2,0:T(4,128)S(1)}, s32[1,48,4]{1,2,0:T(4,128)}, u32[]{:S(2)}) copy-start(s32[1,48,4]{1,2,0:T(4,128)} %param.16) | copy-start | bytes 2308
  169.0 30.9 %copy-start.16 = (f32[1,48,4]{1,2,0:T(4,128)S(1)}, f32[1,48,4]{1,2,0:T(4,128)}, u32[]{:S(2)}) copy-start(f32[1,48,4]{1,2,0:T(4,128)} %param.17) | copy-start | bytes 2308
  193.7 31.8 %all-to-all-start.6 = ((f32[16,48,3,128]{3,1,2,0:T(8,128)}), f32[16,48,3,128]{3,1,2,0:T(8,128)S(1)}, u32[]{:S(2)}, u32[]{:S(2)}) async-start(f32[16,48,3,128]{3,1,2,0:T(8,128)} %copy.67), calls=%async_computation.6 | async-start | bytes 2359296 | tf_op jit(solution)/shard_map/all_to_all | solution.py:64
  225.6 0.7 copy-start.13
  226.3 5.2 %copy-start.11 = (bf16[3,1024,128]{2,1,0:T(8,128)(2,1)S(1)}, bf16[3,1024,128]{2,1,0:T(8,128)(2,1)}, u32[]{:S(2)}) copy-start(bf16[3,1024,128]{2,1,0:T(8,128)(2,1)} %get-tuple-element.101) | copy-start | bytes 2359300
  230.2 31.7 %collective-permute-start = (bf16[128,6144]{1,0:T(8,128)(2,1)}, bf16[128,6144]{1,0:T(8,128)(2,1)S(1)}, u32[]{:S(2)}, u32[]{:S(2)}) collective-permute-start(bf16[128,6144]{1,0:T(8,128)(2,1)} %convolution_convert_fusion), channel_id=1, source_target_pairs={{1,0},{3,2},{5,4},{7,6},{9,8},{11,10},{13,12},{15,14},{17,16},{19,... | collective-permute-start | bytes 4718600 | tf_op jit(solution)/shard_map/ppermute | solution.py:14
where the time goes:
time: 265 us; the launch traced here: 263 us
  waiting for transfers between devices  111 us (42%)
  local copies, waits for them, and re-layouts  42 us (16%)
  matrix products  41.8 us (16%)
  starting transfers between devices  33.8 us (13%)
  blocking collectives  28.3 us (11%)
  other arithmetic  5.17 us (2%)
    all_to_all x1, blocking collectives, per_device(): lax.all_to_all(query_back, 'seq', split_axis=0, concat_axis=0, tiled=True)  28.3 us
    all_to_all x1, waiting for transfers between devices, owner_rows(): lax.all_to_all(key_parts, 'seq', split_axis=0, concat_axis=0, tiled=True)  24.7 us
    all_to_all x1, waiting for transfers between devices, owner_rows(): lax.all_to_all(value_parts, 'seq', split_axis=0, concat_axis=0, tiled=True)  23.8 us
    all_to_all x1, waiting for transfers between devices, per_device(): lax.all_to_all(token_layout(dout[0]), 'seq', split_axis=0, concat_axis=0,...  16.8 us
    all_to_all x1, waiting for transfers between devices, per_device(): lax.all_to_all(token_layout(query[0]), 'seq', split_axis=0, concat_axis=0...  16.4 us
    all_to_all x1, waiting for transfers between devices, per_device(): lax.all_to_all(memory_layout(key_used), 'seq', split_axis=0, concat_axis=...  15.7 us
    all_to_all x1, waiting for transfers between devices, per_device(): lax.all_to_all(memory_layout(value_used), 'seq', split_axis=0, concat_axi...  13.1 us
    dot_general x6, matrix products, visit_block(): jnp.dot(scores_grad, key_head, preferred_element_type=jnp.float32)  11.7 us
  transfers between devices with their start and end apart: 7, of which 6 were waited for; matrix products, arithmetic and copies ran while one was open for 5% of the time, Pallas kernels for 0%

commit v1 on v0

--- a/solution.py
+++ b/solution.py
@@ -3,9 +3,15 @@
 import jax
 import jax.numpy as jnp
 from jax import lax
+from jax.experimental import pallas as pl
+from jax.experimental.pallas import tpu as pltpu
 from jax.sharding import PartitionSpec as P
 
 HEAD_DIM = 128
+LIVE = 256
+HALF = LIVE // 2
+BF = jnp.bfloat16
+F32 = jnp.float32
 
 
 def passed_along(block, axis, distance):
@@ -155,9 +161,340 @@
     return (dquery, dkey_tok, dvalue_tok)
 
 
+def copy_to(src, dst, send_sem, recv_sem, seq, span):
+    return pltpu.make_async_remote_copy(
+        src_ref=src,
+        dst_ref=dst,
+        send_sem=send_sem,
+        recv_sem=recv_sem,
+        device_id={"seq": seq, "span": span},
+        device_id_type=pl.DeviceIdType.MESH,
+    )
+
+
+def fused_kernel(
+    q_ref, g_ref, k_ref, v_ref, idx_ref, idxt_ref, slot_ref, weight_ref,
+    dq_ref, dk_ref, dv_ref,
+    kvin, rows, kv, acc, out16, ra, rb, r2a, r2b, r2send, r3, r3send, back_send, back,
+    pool_send, pool_got,
+    a_send, a_recv, z_send, xy_send, f_send, kv_recv,
+    r1_send, ra_recv, rb_recv, r2_send, r2_recv, r3_send, r3_recv,
+    b_send, b_recv, p_send, p_recv,
+):
+    n = 16
+    me = lax.axis_index("seq")
+    span = lax.axis_index("span")
+    other = 1 - span
+    capacity = k_ref.shape[0]
+    cols = kv.shape[3]
+    z, y, x = me // 4, (me // 2) % 2, me % 2
+    xn = me + 1 - 2 * x
+    yn = me + 2 - 4 * y
+    own_line = me % 4
+    x_line = xn % 4
+    y_line = yn % 4
+    d_line = 3 - own_line
+    scale = HEAD_DIM ** (-0.5)
+
+    barrier = pltpu.get_barrier_semaphore()
+    for off in range(1, n):
+        pl.semaphore_signal(
+            barrier, inc=1, device_id={"seq": (me + off) % n, "span": span},
+            device_id_type=pl.DeviceIdType.MESH,
+        )
+    for off in range(n):
+        pl.semaphore_signal(
+            barrier, inc=1, device_id={"seq": (me + off) % n, "span": other},
+            device_id_type=pl.DeviceIdType.MESH,
+        )
+    for p in range(n // 2):
+        kvin[p] = k_ref[:, p * cols : (p + 1) * cols]
+        kvin[n // 2 + p] = v_ref[:, p * cols : (p + 1) * cols]
+    pl.semaphore_wait(barrier, 2 * n - 1)
+
+    def spread(off):
+        p = (me + off) % n
+        return copy_to(kvin.at[p], rows.at[me], a_send.at[off], a_recv.at[me], p, span)
+
+    for off in range(1, n):
+        spread(off).start()
+    rows[me] = kvin[me]
+
+    @pl.when(span == 1)
+    def _():
+        lanes = lax.broadcasted_iota(jnp.int32, pool_send.shape, 1)
+        total = jnp.zeros(pool_send.shape, F32)
+        for j in range(slot_ref.shape[1]):
+            total = total + jnp.where(lanes == slot_ref[:, j : j + 1], weight_ref[:, j : j + 1], 0.0)
+        pool_send[...] = total
+        copy_to(pool_send, pool_got, p_send, p_recv, me, other).start()
+
+    picks = lax.broadcasted_iota(jnp.int32, (LIVE, n * capacity), 0) == idx_ref[...]
+    picks = jnp.where(picks, 1.0, 0.0).astype(BF)
+    for off in range(1, n):
+        p = (me + off) % n
+        copy_to(kvin.at[p], rows.at[p], a_send.at[off], a_recv.at[p], p, span).wait_recv()
+    packed = jnp.dot(picks, rows[...].reshape(n * capacity, cols), preferred_element_type=F32)
+    kv[me] = packed.astype(BF).reshape(2, HALF, cols)
+
+    def move(block, half, sem, target):
+        return copy_to(kv.at[block, half], kv.at[block, half], sem, kv_recv.at[block, half], target, span)
+
+    def arrived(block, half):
+        move(block, half, z_send.at[0, 0], xn).wait_recv()
+
+    def along_z(k):
+        return ((z + k) % 4) * 4 + own_line
+
+    for half in range(2):
+        for k in (1, 3, 2):
+            move(me, half, z_send.at[k, half], along_z(k)).start()
+    for k in (0, 1, 3, 2):
+        block = along_z(k)
+        if k:
+            arrived(block, 0)
+            arrived(block, 1)
+        move(block, 0, xy_send.at[k, 0, 0], xn).start()
+        move(block, 1, xy_send.at[k, 1, 1], yn).start()
+        move(block, 1, xy_send.at[k, 0, 1], xn).start()
+        move(block, 0, xy_send.at[k, 1, 0], yn).start()
+
+    def compute_line(line):
+        def triple(zz, carry):
+            t = zz * 4 + line
+            start = pl.multiple_of(t * cols, 128)
+            for h in range(cols // HEAD_DIM):
+                here = pl.ds(pl.multiple_of(start + h * HEAD_DIM, 128), HEAD_DIM)
+                inner = slice(h * HEAD_DIM, (h + 1) * HEAD_DIM)
+                query = q_ref[:, here]
+                grad = g_ref[:, here]
+                key = kv[t, :, :, inner].reshape(LIVE, HEAD_DIM)
+                value = kv[t + 8, :, :, inner].reshape(LIVE, HEAD_DIM)
+                last = (((1,), (1,)), ((), ()))
+                first = (((0,), (0,)), ((), ()))
+                scores = lax.dot_general(query, key, last, preferred_element_type=F32) * scale
+                shifted = jnp.exp(scores - jnp.max(scores, axis=1, keepdims=True))
+                probs = shifted / jnp.sum(shifted, axis=1, keepdims=True)
+                low = probs.astype(BF)
+                probs_grad = lax.dot_general(grad, value, last, preferred_element_type=F32)
+                delta = jnp.sum(low.astype(F32) * probs_grad, axis=1, keepdims=True)
+                scores_grad = (probs * (probs_grad - delta)).astype(BF)
+                dq = jnp.dot(scores_grad, key, preferred_element_type=F32) * scale
+                dq_ref[:, here] = dq.astype(BF)
+
+                @pl.when(span == 1)
+                def _():
+                    dkey = lax.dot_general(scores_grad, query, first, preferred_element_type=F32)
+                    dkey = (dkey * scale).reshape(2, HALF, HEAD_DIM)
+                    dvalue = lax.dot_general(low, grad, first, preferred_element_type=F32)
+                    dvalue = dvalue.reshape(2, HALF, HEAD_DIM)
+                    acc[t, :, :, inner] = dkey
+                    acc[t + 8, :, :, inner] = dvalue
+                    out16[t, :, :, inner] = dkey.astype(BF)
+                    out16[t + 8, :, :, inner] = dvalue.astype(BF)
+
+            return carry
+
+        lax.fori_loop(0, 2, triple, 0)
+
+    def send_a(line, slot, zz):
+        return copy_to(
+            out16.at[zz * 4 + line, 0], ra.at[slot, zz], r1_send.at[0, slot, zz], ra_recv.at[slot, zz], yn, span
+        )
+
+    def send_b(line, slot, zz):
+        return copy_to(
+            out16.at[zz * 4 + line, 1], rb.at[slot, zz], r1_send.at[1, slot, zz], rb_recv.at[slot, zz], xn, span
+        )
+
+    compute_line(own_line)
+    for zz in (0, 1, 2, 3):
+        bx, by = zz * 4 + x_line, zz * 4 + y_line
+        arrived(bx, 0)
+        move(bx, 0, f_send.at[zz, 0], yn).start()
+        arrived(by, 1)
+        move(by, 1, f_send.at[zz, 1], xn).start()
+    for zz in range(4):
+        arrived(zz * 4 + x_line, 1)
+    compute_line(x_line)
+
+    @pl.when(span == 1)
+    def _():
+        for zz in range(4):
+            send_b(x_line, 0, zz).start()
+
+    for zz in range(4):
+        arrived(zz * 4 + y_line, 0)
+    compute_line(y_line)
+
+    @pl.when(span == 1)
+    def _():
+        for zz in range(4):
+            send_a(y_line, 0, zz).start()
+
+    for zz in range(4):
+        for half in range(2):
+            arrived(zz * 4 + d_line, half)
+    compute_line(d_line)
+
+    def second(zz, side):
+        if side == 0:
+            return copy_to(r2send.at[zz, 0], r2a.at[zz], r2_send.at[zz, 0], r2_recv.at[zz, 0], xn, span)
+        return copy_to(r2send.at[zz, 1], r2b.at[zz], r2_send.at[zz, 1], r2_recv.at[zz, 1], yn, span)
+
+    def third(k):
+        return copy_to(r3send.at[k], r3.at[k], r3_send.at[k], r3_recv.at[k], along_z(k), span)
+
+    def give(off):
+        p = (me + off) % n
+        return copy_to(back_send.at[p], back.at[me], b_send.at[off], b_recv.at[me], p, other)
+
+    @pl.when(span == 1)
+    def _():
+        for zz in range(4):
+            send_a(d_line, 1, zz).start()
+            send_b(d_line, 1, zz).start()
+        for zz in range(4):
+            send_a(d_line, 1, zz).wait_recv()
+            r2send[zz, 0] = (acc[zz * 4 + x_line, 0] + ra[1, zz].astype(F32)).astype(BF)
+            second(zz, 0).start()
+            send_b(d_line, 1, zz).wait_recv()
+            r2send[zz, 1] = (acc[zz * 4 + y_line, 1] + rb[1, zz].astype(F32)).astype(BF)
+            second(zz, 1).start()
+        for zz in range(4):
+            send_a(y_line, 0, zz).wait_recv()
+            send_b(x_line, 0, zz).wait_recv()
+            second(zz, 0).wait_recv()
+            second(zz, 1).wait_recv()
+
+        def line_total(k, half):
+            zz = (z + k) % 4
+            if half == 0:
+                return acc[zz * 4 + own_line, 0] + ra[0, zz].astype(F32) + r2a[zz].astype(F32)
+            return acc[zz * 4 + own_line, 1] + rb[0, zz].astype(F32) + r2b[zz].astype(F32)
+
+        for k in (2, 1, 3):
+            for half in range(2):
+                r3send[k, half] = line_total(k, half).astype(BF)
+            third(k).start()
+        for k in (1, 3, 2):
+            third(k).wait_recv()
+        total = []
+        for half in range(2):
+            mine = line_total(0, half)
+            for k in (1, 2, 3):
+                mine = mine + r3[k, half].astype(F32)
+            total.append(mine.astype(BF))
+        summed = jnp.concatenate(total, axis=0)
+        spots = lax.broadcasted_iota(jnp.int32, (n * capacity, LIVE), 1) == idxt_ref[...]
+        spots = jnp.where(spots, 1.0, 0.0).astype(BF)
+        wide = jnp.dot(spots, summed, preferred_element_type=F32).astype(BF)
+        back_send[...] = wide.reshape(n, capacity, cols)
+        for off in range(n):
+            give(off).start()
+        dk_ref[...] = jnp.zeros(dk_ref.shape, BF)
+        dv_ref[...] = jnp.zeros(dv_ref.shape, BF)
+
+    @pl.when(span == 0)
+    def _():
+        copy_to(pool_send, pool_got, p_send, p_recv, me, other).wait_recv()
+        matrix = pool_got[...]
+        for p in range(n):
+            copy_to(back_send.at[p], back.at[p], b_send.at[p], b_recv.at[p], me, other).wait_recv()
+            tokens = lax.dot_general(
+                matrix, back[p].astype(F32), (((0,), (0,)), ((), ())),
+                precision=lax.Precision.HIGHEST, preferred_element_type=F32,
+            ).astype(BF)
+            if p < n // 2:
+                dk_ref[:, p * cols : (p + 1) * cols] = tokens
+            else:
+                q = p - n // 2
+                dv_ref[:, q * cols : (q + 1) * cols] = tokens
+
+    for off in range(1, n):
+        spread(off).wait_send()
+    for half in range(2):
+        for k in range(1, 4):
+            move(me, half, z_send.at[k, half], along_z(k)).wait_send()
+    for k in range(4):
+        block = along_z(k)
+        for half in range(2):
+            move(block, half, xy_send.at[k, 0, half], xn).wait_send()
+            move(block, half, xy_send.at[k, 1, half], yn).wait_send()
+        move(k * 4 + x_line, 0, f_send.at[k, 0], yn).wait_send()
+        move(k * 4 + y_line, 1, f_send.at[k, 1], xn).wait_send()
+
+    @pl.when(span == 1)
+    def _():
+        copy_to(pool_send, pool_got, p_send, p_recv, me, other).wait_send()
+        for zz in range(4):
+            send_b(x_line, 0, zz).wait_send()
+            send_a(y_line, 0, zz).wait_send()
+            send_a(d_line, 1, zz).wait_send()
+            send_b(d_line, 1, zz).wait_send()
+            second(zz, 0).wait_send()
+            second(zz, 1).wait_send()
+        for k in range(1, 4):
+            third(k).wait_send()
+        for off in range(n):
+            give(off).wait_send()
+
+
+def per_device_fused(query, dout, mem_key, mem_value, keep_count, keep_slot, pool_weight):
+    n = 16
+    tokens, width = query.shape[1:]
+    capacity = mem_key.shape[1]
+    cols = 2 * width // n
+    counts = keep_count[0]
+    ends = jnp.cumsum(counts)
+    within = jnp.arange(capacity, dtype=jnp.int32)
+    place = jnp.where(
+        within[None, :] < counts[:, None], (ends - counts)[:, None] + within[None, :], -1
+    ).reshape(1, n * capacity)
+    vmem = pl.BlockSpec(memory_space=pltpu.VMEM)
+    dma = pltpu.SemaphoreType.DMA
+    out = jax.ShapeDtypeStruct((tokens, width), BF)
+    half = (HALF, cols)
+    dq, dk, dv = pl.pallas_call(
+        fused_kernel,
+        out_shape=(out, out, out),
+        in_specs=[vmem] * 8,
+        out_specs=(vmem, vmem, vmem),
+        scratch_shapes=[
+            pltpu.VMEM((n, capacity, cols), BF),
+            pltpu.VMEM((n, capacity, cols), BF),
+            pltpu.VMEM((n, 2) + half, BF),
+            pltpu.VMEM((n, 2) + half, F32),
+            pltpu.VMEM((n, 2) + half, BF),
+            pltpu.VMEM((2, 4) + half, BF),
+            pltpu.VMEM((2, 4) + half, BF),
+            pltpu.VMEM((4,) + half, BF),
+            pltpu.VMEM((4,) + half, BF),
+            pltpu.VMEM((4, 2) + half, BF),
+            pltpu.VMEM((4, 2) + half, BF),
+            pltpu.VMEM((4, 2) + half, BF),
+            pltpu.VMEM((n, capacity, cols), BF),
+            pltpu.VMEM((n, capacity, cols), BF),
+            pltpu.VMEM((capacity, tokens), F32),
+            pltpu.VMEM((capacity, tokens), F32),
+            dma((n,)), dma((n,)), dma((4, 2)), dma((4, 2, 2)), dma((4, 2)), dma((n, 2)),
+            dma((2, 2, 4)), dma((2, 4)), dma((2, 4)), dma((4, 2)), dma((4, 2)), dma((4,)), dma((4,)),
+            dma((n,)), dma((n,)), dma, dma,
+        ],
+        compiler_params=pltpu.CompilerParams(
+            collective_id=0, has_side_effects=True, vmem_limit_bytes=48 << 20
+        ),
+    )(
+        query[0], dout[0], mem_key[0], mem_value[0], place, place.reshape(n * capacity, 1),
+        keep_slot[0], pool_weight[0],
+    )
+    return dq[None], dk[None], dv[None]
+
+
 def solution(mesh):
+    fused = mesh.shape["seq"] == 16 and mesh.shape["span"] == 2
     return jax.shard_map(
-        per_device,
+        per_device_fused if fused else per_device,
         mesh=mesh,
         in_specs=(
             P("span", "seq", None),

time: 265 us -> 105 us (0.40)
  the two profiles are of different devices: /device:TPU:0 before, /device:TPU:30 now
where the time goes in v1:
time: 105 us; the launch traced here: 104 us
  Pallas kernels  93.6 us (89%)
  local copies, waits for them, and re-layouts  8.42 us (8%)
  other arithmetic  1.54 us (1%)
    pallas_call x1, Pallas kernels, per_device_fused(): pl.pallas_call(fused_kernel, out_shape=(out, out, out), in_specs=[vmem] *...  93.6 us
    unnamed x13, local copies, waits for them, and re-layouts  7.4 us

profile of v1, /device:TPU:30, one launch (start us, length us, event | category | flops | bytes accessed | tf_op | source)
XLA Modules:
  0.0 104.3 jit_solution(10974439102421574210)
XLA Ops:
  0.6 0.0 copy-start.2
  0.6 0.8 copy.13
  1.5 0.1 reduce
  1.6 0.7 bitcast_subtract_fusion
  2.2 0.7 add_select_fusion
  3.0 0.1 select_n.25.idx_ref
  3.0 0.8 copy.14
  3.8 0.8 copy.15
  4.6 0.2 select_n.27.idxt_ref
  4.8 0.0 copy-done.2
  4.8 0.0 copy-start
  4.8 1.1 %copy-done = bf16[1,128,3072]{2,1,0:T(8,128)(2,1)S(1)} copy-done((bf16[1,128,3072]{2,1,0:T(8,128)(2,1)S(1)}, bf16[1,128,3072]{2,1,0:T(8,128)(2,1)}, u32[]{:S(2)}) %copy-start) | copy-done | bytes 786456
  5.9 0.0 copy-start.1
  5.9 1.1 %copy-done.1 = bf16[1,128,3072]{2,1,0:T(8,128)(2,1)S(1)} copy-done((bf16[1,128,3072]{2,1,0:T(8,128)(2,1)S(1)}, bf16[1,128,3072]{2,1,0:T(8,128)(2,1)}, u32[]{:S(2)}) %copy-start.1) | copy-done | bytes 786456
  7.0 0.0 copy-start.3
  7.0 1.0 copy-done.3
  8.0 93.6 %shard_map.94 = (bf16[128,3072]{1,0:T(8,128)(2,1)S(1)}, bf16[128,3072]{1,0:T(8,128)(2,1)S(1)}, bf16[128,3072]{1,0:T(8,128)(2,1)S(1)}) custom-call(bf16[128,3072]{1,0:T(8,128)(2,1)S(1)} %bitcast.15, bf16[128,3072]{1,0:T(8,128)(2,1)S(1)} %bitcast.16, bf16[48,3072]{1,0:T(8,128)(2,1)S(1)} %bitcast.17, bf16[48,3072]{1,0:T(8,128)(2,1)S(1)} %bitcast.18, ...), custom_call_target="tpu_custom_call" | custom-call | tf_op jit(solution)/shard_map/pallas_call | solution.py:458
  101.6 0.9 copy.20
  102.5 0.9 copy.21
  103.4 0.9 copy.22
  (1 shorter events, 0.0 us)
Async XLA Ops:
  0.6 4.1 %copy-start.2 = (bf16[1,48,3072]{2,1,0:T(8,128)(2,1)S(1)}, bf16[1,48,3072]{2,1,0:T(8,128)(2,1)}, u32[]{:S(2)}) copy-start(bf16[1,48,3072]{2,1,0:T(8,128)(2,1)} %param.9) | copy-start | bytes 884740
  4.8 1.1 %copy-start = (bf16[1,128,3072]{2,1,0:T(8,128)(2,1)S(1)}, bf16[1,128,3072]{2,1,0:T(8,128)(2,1)}, u32[]{:S(2)}) copy-start(bf16[1,128,3072]{2,1,0:T(8,128)(2,1)} %param.7) | copy-start | bytes 2359300
  5.9 1.1 %copy-start.1 = (bf16[1,128,3072]{2,1,0:T(8,128)(2,1)S(1)}, bf16[1,128,3072]{2,1,0:T(8,128)(2,1)}, u32[]{:S(2)}) copy-start(bf16[1,128,3072]{2,1,0:T(8,128)(2,1)} %param.8) | copy-start | bytes 2359300
  7.0 1.0 copy-start.3

commit v2 on v0

--- a/solution.py
+++ b/solution.py
@@ -3,9 +3,17 @@
 import jax
 import jax.numpy as jnp
 from jax import lax
+from jax.experimental import pallas as pl
+from jax.experimental.pallas import tpu as pltpu
 from jax.sharding import PartitionSpec as P
 
 HEAD_DIM = 128
+LIVE = 256
+HALF = LIVE // 2
+BF = jnp.bfloat16
+F32 = jnp.float32
+THIRD = F32
+BACK = F32
 
 
 def passed_along(block, axis, distance):
@@ -155,9 +163,416 @@
     return (dquery, dkey_tok, dvalue_tok)
 
 
+def copy_to(src, dst, send_sem, recv_sem, seq, span):
+    return pltpu.make_async_remote_copy(
+        src_ref=src,
+        dst_ref=dst,
+        send_sem=send_sem,
+        recv_sem=recv_sem,
+        device_id={"seq": seq, "span": span},
+        device_id_type=pl.DeviceIdType.MESH,
+    )
+
+
+def fused_kernel(
+    q_hbm, g_hbm, k_hbm, v_hbm, count_ref, slot_ref, weight_ref,
+    dq_ref, dk_ref, dv_ref,
+    q_ref, g_ref, k_ref, v_ref, picks_ref,
+    kvin, rows, kv, acc, out16, ra, rb, r2a, r2b, r2send, r3, r3send, back_send, back,
+    pool_send, pool_got,
+    in_sem, a_send, a_recv, z_send, z_recv, xy_send, f_send, kv_recv,
+    r1_send, ra_recv, rb_recv, r2_send, r2_recv, r3_send, r3_recv,
+    b_send, b_recv, p_send, p_recv,
+):
+    n = 16
+    parts = kv.shape[0]
+    wide = HEAD_DIM
+    me = lax.axis_index("seq")
+    span = lax.axis_index("span")
+    other = 1 - span
+    capacity = k_ref.shape[0]
+    z, y, x = me // 4, (me // 2) % 2, me % 2
+    xn = me + 1 - 2 * x
+    yn = me + 2 - 4 * y
+    own_line = me % 4
+    x_line = xn % 4
+    y_line = yn % 4
+    d_line = 3 - own_line
+    scale = HEAD_DIM ** (-0.5)
+    last = (((1,), (1,)), ((), ()))
+    first = (((0,), (0,)), ((), ()))
+
+    loads = [
+        pltpu.make_async_copy(src, dst, in_sem.at[i])
+        for i, (src, dst) in enumerate(((k_hbm, k_ref), (v_hbm, v_ref), (q_hbm, q_ref), (g_hbm, g_ref)))
+    ]
+    for load in loads:
+        load.start()
+    barrier = pltpu.get_barrier_semaphore()
+    for off in range(1, n):
+        pl.semaphore_signal(
+            barrier, inc=1, device_id={"seq": (me + off) % n, "span": span},
+            device_id_type=pl.DeviceIdType.MESH,
+        )
+    for off in range(n):
+        pl.semaphore_signal(
+            barrier, inc=1, device_id={"seq": (me + off) % n, "span": other},
+            device_id_type=pl.DeviceIdType.MESH,
+        )
+    loads[0].wait()
+    loads[1].wait()
+    for part in range(parts):
+        for p in range(n // 2):
+            here = slice((p * parts + part) * wide, (p * parts + part + 1) * wide)
+            kvin[part, p] = k_ref[:, here]
+            kvin[part, n // 2 + p] = v_ref[:, here]
+    pl.semaphore_wait(barrier, 2 * n - 1)
+
+    def spread(part, off):
+        p = (me + off) % n
+        return copy_to(kvin.at[part, p], rows.at[part, me], a_send.at[part, off], a_recv.at[part, me], p, span)
+
+    for part in range(parts):
+        for off in range(1, n):
+            spread(part, off).start()
+        rows[part, me] = kvin[part, me]
+
+    @pl.when(span == 1)
+    def _():
+        spots = lax.broadcasted_iota(jnp.int32, pool_send.shape, 0)
+        total = jnp.zeros(pool_send.shape, F32)
+        for j in range(slot_ref.shape[0]):
+            total = total + jnp.where(spots == slot_ref[j : j + 1, :], weight_ref[j : j + 1, :], 0.0)
+        pool_send[...] = total
+        copy_to(pool_send, pool_got, p_send, p_recv, me, other).start()
+
+    slots = n * capacity
+    counts = jnp.broadcast_to(count_ref[...], (8, n)).astype(F32).astype(BF)
+    owner = lax.broadcasted_iota(jnp.int32, (n, slots), 1)
+    below = lax.broadcasted_iota(jnp.int32, (n, slots), 0) * capacity
+    ahead = jnp.where(owner >= below + capacity, 1.0, 0.0).astype(BF)
+    inside = jnp.where((owner >= below) & (owner < below + capacity), 1.0, 0.0).astype(BF)
+    position = jnp.where((owner >= below) & (owner < below + capacity), owner - below, 0)
+    position = jnp.sum(position.astype(F32), axis=0, keepdims=True)
+    offset = jnp.dot(counts, ahead, preferred_element_type=F32)[:1]
+    length = jnp.dot(counts, inside, preferred_element_type=F32)[:1]
+    place = jnp.where(position < length, offset + position, -1.0).astype(jnp.int32)
+    picks = lax.broadcasted_iota(jnp.int32, (LIVE, slots), 0) == place
+    picks_ref[...] = jnp.where(picks, 1.0, 0.0).astype(BF)
+
+    def along_z(k):
+        return ((z + k) % 4) * 4 + own_line
+
+    def column(part, k):
+        mine = kv.at[part, own_line, :, z]
+        return copy_to(mine, mine, z_send.at[part, k], z_recv.at[part, z], along_z(k), span)
+
+    def column_in(part, k):
+        block = kv.at[part, own_line, :, (z + k) % 4]
+        return copy_to(block, block, z_send.at[part, k], z_recv.at[part, (z + k) % 4], along_z(k), span)
+
+    def line_move(part, line, half, sem, target):
+        block = kv.at[part, line, half]
+        return copy_to(block, block, sem, kv_recv.at[part, line, half], target, span)
+
+    def to_x(part, half):
+        return line_move(part, own_line, half, xy_send.at[part, 0, half], xn)
+
+    def to_y(part, half):
+        return line_move(part, own_line, half, xy_send.at[part, 1, half], yn)
+
+    def onward_y(part):
+        return line_move(part, x_line, 0, f_send.at[part, 0], yn)
+
+    def onward_x(part):
+        return line_move(part, y_line, 1, f_send.at[part, 1], xn)
+
+    def arrived(part, line, half):
+        line_move(part, line, half, f_send.at[part, 0], xn).wait_recv()
+
+    def pack(part):
+        for off in range(1, n):
+            p = (me + off) % n
+            copy_to(kvin.at[part, p], rows.at[part, p], a_send.at[part, off], a_recv.at[part, p], p, span).wait_recv()
+        packed = jnp.dot(picks_ref[...], rows[part].reshape(slots, wide), preferred_element_type=F32)
+        kv[part, own_line, :, z] = packed.astype(BF).reshape(2, HALF, wide)
+        for k in (2, 1, 3):
+            column(part, k).start()
+
+    def share(part):
+        for k in (1, 3, 2):
+            column_in(part, k).wait_recv()
+        to_x(part, 0).start()
+        to_y(part, 1).start()
+        to_x(part, 1).start()
+        to_y(part, 0).start()
+
+    def forward(part):
+        arrived(part, x_line, 0)
+        onward_y(part).start()
+        arrived(part, y_line, 1)
+        onward_x(part).start()
+
+    def send_a(part, line, slot):
+        return copy_to(
+            out16.at[part, line, 0], ra.at[part, slot], r1_send.at[part, 0, slot], ra_recv.at[part, slot], yn, span
+        )
+
+    def send_b(part, line, slot):
+        return copy_to(
+            out16.at[part, line, 1], rb.at[part, slot], r1_send.at[part, 1, slot], rb_recv.at[part, slot], xn, span
+        )
+
+    def compute_line(part, line):
+        def triple(zz, carry):
+            start = ((zz * 4 + line) * parts + part) * wide
+            here = pl.ds(pl.multiple_of(start, 128), wide)
+            query = q_ref[:, here]
+            grad = g_ref[:, here]
+            key = kv[part, line, :, zz].reshape(LIVE, wide)
+            value = kv[part, line, :, zz + 2].reshape(LIVE, wide)
+            scores = lax.dot_general(query, key, last, preferred_element_type=F32) * scale
+            shifted = jnp.exp(scores - jnp.max(scores, axis=1, keepdims=True))
+            probs = shifted / jnp.sum(shifted, axis=1, keepdims=True)
+            low = probs.astype(BF)
+            probs_grad = lax.dot_general(grad, value, last, preferred_element_type=F32)
+            delta = jnp.sum(low.astype(F32) * probs_grad, axis=1, keepdims=True)
+            scores_grad = (probs * (probs_grad - delta)).astype(BF)
+            dq = jnp.dot(scores_grad, key, preferred_element_type=F32) * scale
+            dq_ref[:, here] = dq.astype(BF)
+
+            @pl.when(span == 1)
+            def _():
+                dkey = lax.dot_general(scores_grad, query, first, preferred_element_type=F32)
+                dkey = (dkey * scale).reshape(2, HALF, wide)
+                dvalue = lax.dot_general(low, grad, first, preferred_element_type=F32)
+                dvalue = dvalue.reshape(2, HALF, wide)
+                acc[part, line, :, zz] = dkey
+                acc[part, line, :, zz + 2] = dvalue
+                out16[part, line, :, zz] = dkey.astype(BF)
+                out16[part, line, :, zz + 2] = dvalue.astype(BF)
+
+            return carry
+
+        lax.fori_loop(0, 2, triple, 0, unroll=True)
+
+    def compute(part):
+        compute_line(part, own_line)
+        arrived(part, x_line, 1)
+        compute_line(part, x_line)
+
+        @pl.when(span == 1)
+        def _():
+            send_b(part, x_line, 0).start()
+
+        arrived(part, y_line, 0)
+        compute_line(part, y_line)
+
+        @pl.when(span == 1)
+        def _():
+            send_a(part, y_line, 0).start()
+
+        arrived(part, d_line, 0)
+        arrived(part, d_line, 1)
+        compute_line(part, d_line)
+
+        @pl.when(span == 1)
+        def _():
+            send_a(part, d_line, 1).start()
+            send_b(part, d_line, 1).start()
+
+    def second_a(part):
+        return copy_to(r2send.at[part, 0], r2a.at[part], r2_send.at[part, 0], r2_recv.at[part, 0], xn, span)
+
+    def second_b(part):
+        return copy_to(r2send.at[part, 1], r2b.at[part], r2_send.at[part, 1], r2_recv.at[part, 1], yn, span)
+
+    def reduce_second(part):
+        @pl.when(span == 1)
+        def _():
+            send_a(part, d_line, 1).wait_recv()
+            r2send[part, 0] = (acc[part, x_line, 0] + ra[part, 1].astype(F32)).astype(BF)
+            second_a(part).start()
+            send_b(part, d_line, 1).wait_recv()
+            r2send[part, 1] = (acc[part, y_line, 1] + rb[part, 1].astype(F32)).astype(BF)
+            second_b(part).start()
+
+    def third(part, k):
+        return copy_to(
+            r3send.at[part, k], r3.at[part, k], r3_send.at[part, k], r3_recv.at[part, k], along_z(k), span
+        )
+
+    def line_total(part, k):
+        zz = (z + k) % 4
+        upper = acc[part, own_line, 0, zz] + ra[part, 0, zz].astype(F32) + r2a[part, zz].astype(F32)
+        lower = acc[part, own_line, 1, zz] + rb[part, 0, zz].astype(F32) + r2b[part, zz].astype(F32)
+        return jnp.concatenate([upper, lower], axis=0)
+
+    def reduce_third(part):
+        @pl.when(span == 1)
+        def _():
+            send_a(part, y_line, 0).wait_recv()
+            send_b(part, x_line, 0).wait_recv()
+            second_a(part).wait_recv()
+            second_b(part).wait_recv()
+            for k in (2, 1, 3):
+                r3send[part, k] = line_total(part, k).astype(r3send.dtype)
+                third(part, k).start()
+
+    def give(part, off):
+        p = (me + off) % n
+        return copy_to(back_send.at[part, p], back.at[part, me], b_send.at[part, off], b_recv.at[part, me], p, other)
+
+    def hand_back(part):
+        @pl.when(span == 1)
+        def _():
+            total = line_total(part, 0)
+            for k in (1, 3, 2):
+                third(part, k).wait_recv()
+                total = total + r3[part, k].astype(F32)
+            high = total.astype(BF)
+            owned = lax.dot_general(picks_ref[...], high, first, preferred_element_type=F32)
+            if back_send.dtype == F32:
+                rest = (total - high.astype(F32)).astype(BF)
+                owned = owned + lax.dot_general(picks_ref[...], rest, first, preferred_element_type=F32)
+            back_send[part] = owned.astype(back_send.dtype).reshape(n, capacity, wide)
+            for off in range(n):
+                give(part, off).start()
+
+    pack(0)
+    pack(1)
+    share(0)
+    pack(2)
+    share(1)
+    forward(0)
+    loads[2].wait()
+    loads[3].wait()
+    compute(0)
+    share(2)
+    forward(1)
+    compute(1)
+    reduce_second(0)
+    forward(2)
+    reduce_third(0)
+    compute(2)
+    reduce_second(1)
+    hand_back(0)
+    reduce_third(1)
+    reduce_second(2)
+    hand_back(1)
+    reduce_third(2)
+    hand_back(2)
+
+    @pl.when(span == 1)
+    def _():
+        dk_ref[...] = jnp.zeros(dk_ref.shape, BF)
+        dv_ref[...] = jnp.zeros(dv_ref.shape, BF)
+
+    @pl.when(span == 0)
+    def _():
+        copy_to(pool_send, pool_got, p_send, p_recv, me, other).wait_recv()
+        matrix = pool_got[...]
+        for part in range(parts):
+            for p in range(n):
+                copy_to(
+                    back_send.at[part, p], back.at[part, p], b_send.at[part, p], b_recv.at[part, p], me, other
+                ).wait_recv()
+            for p in range(n):
+                tokens = jnp.dot(
+                    matrix, back[part, p].astype(F32),
+                    precision=lax.Precision.HIGHEST, preferred_element_type=F32,
+                ).astype(BF)
+                start = ((p % (n // 2)) * parts + part) * wide
+                if p < n // 2:
+                    dk_ref[:, start : start + wide] = tokens
+                else:
+                    dv_ref[:, start : start + wide] = tokens
+
+    for part in range(parts):
+        for off in range(1, n):
+            spread(part, off).wait_send()
+        for k in (1, 2, 3):
+            column(part, k).wait_send()
+        for half in range(2):
+            to_x(part, half).wait_send()
+            to_y(part, half).wait_send()
+        onward_y(part).wait_send()
+        onward_x(part).wait_send()
+
+    @pl.when(span == 1)
+    def _():
+        copy_to(pool_send, pool_got, p_send, p_recv, me, other).wait_send()
+        for part in range(parts):
+            send_b(part, x_line, 0).wait_send()
+            send_a(part, y_line, 0).wait_send()
+            send_a(part, d_line, 1).wait_send()
+            send_b(part, d_line, 1).wait_send()
+            second_a(part).wait_send()
+            second_b(part).wait_send()
+            for k in (1, 2, 3):
+                third(part, k).wait_send()
+            for off in range(n):
+                give(part, off).wait_send()
+
+
+def per_device_fused(query, dout, mem_key, mem_value, keep_count, keep_slot, pool_weight):
+    n = 16
+    tokens, width = query.shape[1:]
+    capacity = mem_key.shape[1]
+    parts = 2 * width // n // HEAD_DIM
+    vmem = pl.BlockSpec(memory_space=pltpu.VMEM)
+    hbm = pl.BlockSpec(memory_space=pl.ANY)
+    dma = pltpu.SemaphoreType.DMA
+    out = jax.ShapeDtypeStruct((tokens, width), BF)
+    half = (HALF, HEAD_DIM)
+    owned = (parts, n, capacity, HEAD_DIM)
+    dq, dk, dv = pl.pallas_call(
+        fused_kernel,
+        out_shape=(out, out, out),
+        in_specs=[hbm] * 4 + [vmem] * 3,
+        out_specs=(vmem, vmem, vmem),
+        scratch_shapes=[
+            pltpu.VMEM((tokens, width), BF),
+            pltpu.VMEM((tokens, width), BF),
+            pltpu.VMEM((capacity, width), BF),
+            pltpu.VMEM((capacity, width), BF),
+            pltpu.VMEM((LIVE, n * capacity), BF),
+            pltpu.VMEM(owned, BF),
+            pltpu.VMEM(owned, BF),
+            pltpu.VMEM((parts, 4, 2, 4) + half, BF),
+            pltpu.VMEM((parts, 4, 2, 4) + half, F32),
+            pltpu.VMEM((parts, 4, 2, 4) + half, BF),
+            pltpu.VMEM((parts, 2, 4) + half, BF),
+            pltpu.VMEM((parts, 2, 4) + half, BF),
+            pltpu.VMEM((parts, 4) + half, BF),
+            pltpu.VMEM((parts, 4) + half, BF),
+            pltpu.VMEM((parts, 2, 4) + half, BF),
+            pltpu.VMEM((parts, 4, LIVE, HEAD_DIM), THIRD),
+            pltpu.VMEM((parts, 4, LIVE, HEAD_DIM), THIRD),
+            pltpu.VMEM(owned, BACK),
+            pltpu.VMEM(owned, BACK),
+            pltpu.VMEM((tokens, capacity), F32),
+            pltpu.VMEM((tokens, capacity), F32),
+            dma((4,)),
+            dma((parts, n)), dma((parts, n)), dma((parts, 4)), dma((parts, 4)), dma((parts, 2, 2)),
+            dma((parts, 2)), dma((parts, 4, 2)),
+            dma((parts, 2, 2)), dma((parts, 2)), dma((parts, 2)), dma((parts, 2)), dma((parts, 2)),
+            dma((parts, 4)), dma((parts, 4)),
+            dma((parts, n)), dma((parts, n)), dma, dma,
+        ],
+        compiler_params=pltpu.CompilerParams(
+            collective_id=0, has_side_effects=True, vmem_limit_bytes=56 << 20
+        ),
+    )(
+        query[0], dout[0], mem_key[0], mem_value[0], keep_count, keep_slot[0].T, pool_weight[0].T,
+    )
+    return dq[None], dk[None], dv[None]
+
+
 def solution(mesh):
+    fused = mesh.shape["seq"] == 16 and mesh.shape["span"] == 2
     return jax.shard_map(
-        per_device,
+        per_device_fused if fused else per_device,
         mesh=mesh,
         in_specs=(
             P("span", "seq", None),

time: 265 us -> 112 us (0.42)
  waiting for transfers between devices: 111 us -> 0 us
  Pallas kernels: 0 us -> 107 us
  matrix products: 41.8 us -> 0 us
  local copies, waits for them, and re-layouts: 42 us -> 4.44 us
  starting transfers between devices: 33.8 us -> 0 us
  blocking collectives: 28.3 us -> 0 us
  other arithmetic: 5.17 us -> 0 us
    all_to_all x6 -> x0, waiting for transfers between devices: 111 us -> none  [the longest x1 24.7 us: owner_rows(): lax.all_to_all(key_parts, 'seq', split_axis=0, concat_axis=0, tiled=True)]
    pallas_call x0 -> x1, Pallas kernels: none -> 107 us  [per_device_fused(): pl.pallas_call(fused_kernel, out_shape=(out, out, out), in_specs=[hbm] *...]
    dot_general x38 -> x0, matrix products: 41.8 us -> none  [the longest x6 11.7 us: visit_block(): jnp.dot(scores_grad, key_head, preferred_element_type=jnp.float32)]
    all_to_all x6 -> x0, starting transfers between devices: 32.5 us -> none  [the longest x1 8.31 us: per_device(): lax.all_to_all(memory_layout(key_used), 'seq', split_axis=0, concat_axis=...]
    all_to_all x1 -> x0, blocking collectives: 28.3 us -> none  [per_device(): lax.all_to_all(query_back, 'seq', split_axis=0, concat_axis=0, tiled=True)]
    squeeze x7 -> x0, local copies, waits for them, and re-layouts: 7.87 us -> none  [the longest x6 7.78 us: per_device(): lax.map(one_head, (query_flat, grad_flat, key_flat, value_flat))]
    dynamic_update_slice x6 -> x0, local copies, waits for them, and re-layouts: 7.85 us -> none  [per_device(): lax.map(one_head, (query_flat, grad_flat, key_flat, value_flat))]
    reshape x9 -> x0, local copies, waits for them, and re-layouts: 5.87 us -> none  [the longest x1 2.39 us: per_device(): jnp.moveaxis(key_grad, 0, 1)]
  transfers between devices with their start and end apart: 7 -> 0, of which waited for: 6 -> 0; matrix products, arithmetic and copies ran while one was open for 5% -> 0% of each run, Pallas kernels for 0% -> 0%
where the time goes in v2:
time: 112 us
  Pallas kernels  107 us (96%)
  local copies, waits for them, and re-layouts  4.44 us (4%)
    pallas_call x1, Pallas kernels, per_device_fused(): pl.pallas_call(fused_kernel, out_shape=(out, out, out), in_specs=[hbm] *...  107 us
    unnamed x7, local copies, waits for them, and re-layouts  4.44 us

profile of v2, /device:TPU:0, one launch (start us, length us, event | category | flops | bytes accessed | tf_op | source)
XLA Modules:
  0.0 111.8 jit_solution(12845257456560777598)
XLA Ops:
  0.6 106.7 %shard_map.94 = (bf16[128,3072]{1,0:T(8,128)(2,1)}, bf16[128,3072]{1,0:T(8,128)(2,1)}, bf16[128,3072]{1,0:T(8,128)(2,1)}) custom-call(bf16[128,3072]{1,0:T(8,128)(2,1)} %bitcast.13, bf16[128,3072]{1,0:T(8,128)(2,1)} %bitcast.14, bf16[48,3072]{1,0:T(8,128)(2,1)} %bitcast.18, bf16[48,3072]{1,0:T(8,128)(2,1)} %bitcast.19, s32[1,16]{1,0:T(1,128)} %count_ref.1, ...), custom_call_target="tpu_custom_call" | custom-call | tf_op jit(solution)/shard_map/pallas_call | solution.py:529
  107.4 0.0 copy-start.1
  107.4 2.1 %copy.13 = bf16[1,128,3072]{2,1,0:T(8,128)(2,1)} copy(bf16[1,128,3072]{2,1,0:T(8,128)(2,1)} %bitcast.17) | data formatting | bytes 1572864
  109.5 0.0 copy-done.1
  109.5 0.0 copy-start
  109.5 0.9 copy.14
  110.4 0.5 copy-done
  111.0 0.9 copy.15
Async XLA Ops:
  107.4 2.1 %copy-start.1 = (bf16[128,3072]{1,0:T(8,128)(2,1)S(1)}, bf16[128,3072]{1,0:T(8,128)(2,1)}, u32[]{:S(2)}) copy-start(bf16[128,3072]{1,0:T(8,128)(2,1)} %get-tuple-element.7) | copy-start | bytes 2359300
  109.5 1.4 %copy-start = (bf16[128,3072]{1,0:T(8,128)(2,1)S(1)}, bf16[128,3072]{1,0:T(8,128)(2,1)}, u32[]{:S(2)}) copy-start(bf16[128,3072]{1,0:T(8,128)(2,1)} %get-tuple-element.8) | copy-start | bytes 2359300

commit v3 on v2

--- a/solution.py
+++ b/solution.py
@@ -440,24 +440,24 @@
                 give(part, off).start()
 
     pack(0)
+    share(0)
     pack(1)
-    share(0)
+    forward(0)
+    share(1)
     pack(2)
-    share(1)
-    forward(0)
+    forward(1)
+    share(2)
     loads[2].wait()
     loads[3].wait()
     compute(0)
-    share(2)
-    forward(1)
+    forward(2)
     compute(1)
     reduce_second(0)
-    forward(2)
+    reduce_second(1)
     reduce_third(0)
     compute(2)
-    reduce_second(1)
+    reduce_third(1)
     hand_back(0)
-    reduce_third(1)
     reduce_second(2)
     hand_back(1)
     reduce_third(2)

time: 112 us -> 104 us (0.929)
  Pallas kernels: 107 us -> 99 us
    pallas_call x1, Pallas kernels: 107 us -> 99 us  [per_device_fused(): pl.pallas_call(fused_kernel, out_shape=(out, out, out), in_specs=[hbm] *...]
where the time goes in v3:
time: 104 us
  Pallas kernels  99 us (95%)
  local copies, waits for them, and re-layouts  4.44 us (4%)
    pallas_call x1, Pallas kernels, per_device_fused(): pl.pallas_call(fused_kernel, out_shape=(out, out, out), in_specs=[hbm] *...  99 us
    unnamed x7, local copies, waits for them, and re-layouts  4.44 us

profile of v3, /device:TPU:0, one launch (start us, length us, event | category | flops | bytes accessed | tf_op | source)
XLA Modules:
  0.0 104.1 jit_solution(17072569408810029005)
XLA Ops:
  0.6 99.0 %shard_map.94 = (bf16[128,3072]{1,0:T(8,128)(2,1)}, bf16[128,3072]{1,0:T(8,128)(2,1)}, bf16[128,3072]{1,0:T(8,128)(2,1)}) custom-call(bf16[128,3072]{1,0:T(8,128)(2,1)} %bitcast.13, bf16[128,3072]{1,0:T(8,128)(2,1)} %bitcast.14, bf16[48,3072]{1,0:T(8,128)(2,1)} %bitcast.18, bf16[48,3072]{1,0:T(8,128)(2,1)} %bitcast.19, s32[1,16]{1,0:T(1,128)} %count_ref.1, ...), custom_call_target="tpu_custom_call" | custom-call | tf_op jit(solution)/shard_map/pallas_call | solution.py:529
  99.6 0.0 copy-start.1
  99.6 2.1 %copy.13 = bf16[1,128,3072]{2,1,0:T(8,128)(2,1)} copy(bf16[1,128,3072]{2,1,0:T(8,128)(2,1)} %bitcast.17) | data formatting | bytes 1572864
  101.8 0.0 copy-done.1
  101.8 0.0 copy-start
  101.8 0.9 copy.14
  102.7 0.5 copy-done
  103.2 0.9 copy.15
Async XLA Ops:
  99.6 2.1 %copy-start.1 = (bf16[128,3072]{1,0:T(8,128)(2,1)S(1)}, bf16[128,3072]{1,0:T(8,128)(2,1)}, u32[]{:S(2)}) copy-start(bf16[128,3072]{1,0:T(8,128)(2,1)} %get-tuple-element.7) | copy-start | bytes 2359300
  101.8 1.4 %copy-start = (bf16[128,3072]{1,0:T(8,128)(2,1)S(1)}, bf16[128,3072]{1,0:T(8,128)(2,1)}, u32[]{:S(2)}) copy-start(bf16[128,3072]{1,0:T(8,128)(2,1)} %get-tuple-element.8) | copy-start | bytes 2359300
